TPU v7x, 256 devices: a whole 4x4x8 slice. The times are simulated.
256 devices in a mesh: dp: 32 (over x, y, core), tensor: 8 (over z).
Axes of the slice: x: 4, y: 4, z: 8, core: 2. Of those that a mesh axis runs over, the one named last changes fastest.
Arguments:
- hidden: bfloat16 [32768, 8192], P(('dp', 'tensor')), may hold values from -50 to 50
- out_weight: bfloat16 [128256, 8192], P(('dp', 'tensor')), may hold values from -1 to 1
- loss_mask: int32 [32768], P(('dp', 'tensor')), may hold values from 0 to 1, as said below
- targets: int32 [32768], P(('dp', 'tensor')), may hold values from 0 to 128255
- kept_count: int32 [256], P(('dp', 'tensor')), may hold values from 0 to 1, as said below
Outputs:
- hidden_grad: bfloat16 [32768, 8192], P(('dp', 'tensor'))
- row_loss: float32 [32768], P(('dp', 'tensor'))
Inputs may be any that keep to these rules, and one draw needn't show every extreme that they name: `loss_mask`: each device's 128 rows hold at least 1 ones. `kept_count`: some entry equals 1 and some entry equals 0.
All inputs are finite; a program needn't handle non-finite values.
Results may differ from a plain program's by a relative error of at most 0.0026.
Values may be sent and summed in bfloat16 or wider, within the bound.
No kernel may reach another device: no remote copies, remote signals or barrier semaphores. Data moves between devices by JAX's collectives and lax.ppermute only.
A program may use at most 128 MiB of HBM per device.

v0:
```python
import jax
import jax.numpy as jnp
from jax import lax
from jax.sharding import PartitionSpec as P

CAP = 1
loss_scale = 128.0


def shards(hidden, out_weight, loss_mask, targets, kept_count):
    order_pos = jnp.cumsum(loss_mask) - 1
    kept_row = (loss_mask == 1) & (order_pos < kept_count[0])
    slot_ids = jnp.arange(CAP, dtype=jnp.int32)
    slot_hits = kept_row[None, :] & (order_pos[None, :] == slot_ids[:, None])
    packed = jnp.dot(
        slot_hits.astype(jnp.bfloat16), hidden, preferred_element_type=jnp.float32
    ).astype(jnp.bfloat16)
    slot_target = jnp.sum(jnp.where(slot_hits, targets[None, :], 0), axis=1)
    packed_target = jnp.where(jnp.any(slot_hits, axis=1), slot_target, -1)
    gathered, gathered_target = (
        lax.all_gather(packed, ("dp", "tensor"), axis=0, tiled=True),
        lax.all_gather(packed_target, ("dp", "tensor"), axis=0, tiled=True),
    )
    filled = gathered_target >= 0
    vocab_rows = out_weight.shape[0]
    device_pos = lax.axis_index(("dp", "tensor"))
    vocab_ids = device_pos * vocab_rows + jnp.arange(vocab_rows, dtype=jnp.int32)
    logits = jnp.einsum("rd,vd->rv", gathered, out_weight, preferred_element_type=jnp.float32)
    target_hit = vocab_ids[None, :] == gathered_target[:, None]
    local_top = jnp.max(logits, axis=1)
    local_pick = jnp.sum(jnp.where(target_hit, logits, 0.0), axis=1)
    row_top = lax.pmax(local_top, ("dp", "tensor"))
    shifted_total = jnp.sum(jnp.exp(logits - row_top[:, None]), axis=1)
    row_total, picked = lax.psum((shifted_total, local_pick), ("dp", "tensor"))
    log_total = row_top + jnp.log(row_total)
    slot_loss = jnp.where(filled, log_total - picked, 0.0)
    probabilities = jnp.exp(logits - log_total[:, None])
    coefficient = jnp.where(
        filled[:, None], probabilities - target_hit.astype(jnp.float32), 0.0
    ).astype(jnp.bfloat16)
    own_grad = lax.psum_scatter(
        jnp.dot(coefficient, out_weight, preferred_element_type=jnp.float32),
        ("dp", "tensor"),
        scatter_dimension=0,
        tiled=True,
    )
    own_grad = own_grad * loss_scale
    own_loss = lax.dynamic_slice_in_dim(slot_loss, device_pos * CAP, CAP, 0)
    slot_pos = jnp.clip(order_pos, 0, CAP - 1)
    hidden_grad = jnp.where(kept_row[:, None], own_grad[slot_pos], 0.0).astype(jnp.bfloat16)
    row_loss = jnp.where(kept_row, own_loss[slot_pos], 0.0)
    return (hidden_grad, row_loss)


def solution(mesh):
    in_specs = (
        P(("dp", "tensor"), None),
        P(("dp", "tensor"), None),
        P(("dp", "tensor")),
        P(("dp", "tensor")),
        P(("dp", "tensor")),
    )
    out_specs = (P(("dp", "tensor"), None), P(("dp", "tensor")))
    return jax.shard_map(shards, mesh=mesh, in_specs=in_specs, out_specs=out_specs, check_vma=False)
```

profile of v0, /device:TPU:97, one launch (start us, length us, event | category | flops | bytes accessed | tf_op | source)
XLA Modules:
  0.0 587.9 jit_solution(10313876143399885499)
XLA Ops:
  7.2 0.0 all-gather.3.cloned.1.call-start
  8.0 0.8 copy.9
  8.8 0.2 reduce-window.4
  8.9 0.1 compare_reduce_fusion
  9.1 1.3 select_reduce_fusion
  10.4 0.4 fusion.11
  10.8 0.6 convert_element_type.16
  11.4 0.0 all-gather.3.cloned.1.call-update
  11.4 0.0 all-reduce.5.cloned.1.call-start
  11.5 0.6 and_reduce_fusion
  13.4 0.1 dynamic-update-slice
  13.5 78.3 %all-reduce = s32[256]{0:T(256)S(1)} all-reduce(s32[256]{0:T(256)S(1)} %dynamic-update-slice), channel_id=1, replica_groups=mesh['dp'=32,'tensor'=8] {'dp','tensor'}, use_global_device_ids=true, to_apply=%add | all-reduce | flops 256 | bytes 2048
  91.8 37.0 %all-gather.3.cloned.1.call-done = bf16[2097152]{0:T(1024)(128)(2,1)} async-done(((bf16[8192]{0:T(1024)(128)(2,1)}), bf16[2097152]{0:T(1024)(128)(2,1)}) %all-gather.3.cloned.1.call-update) | async-done | bytes 4194320 | tf_op jit(solution)/shard_map/all_gather | solution.py:21
  128.8 7.3 %reshape.49 = bf16[256,8192]{1,0:T(8,128)(2,1)} reshape(bf16[2097152]{0:T(1024)(128)(2,1)} %all-gather.3.cloned.1.call-done) | data formatting | bytes 8388608 | tf_op jit(solution)/shard_map/all_gather | solution.py:21
  136.2 6.3 %fusion.15 = (f32[256]{0:T(256)S(1)}, f32[256,501]{0,1:T(8,128)S(1)}) fusion(bf16[256,8192]{1,0:T(8,128)(2,1)} %reshape.49, bf16[501,8192]{1,0:T(8,128)(2,1)} %param.6), kind=kOutput, calls=%fused_computation.29 | convolution fusion | flops 2101474304 | bytes 12916736 | tf_op jit(solution)/shard_map/rd,vd->rv/dot_general | solution.py:28
  142.4 74.6 %pmax.7 = f32[256]{0:T(256)S(1)} all-reduce(f32[256]{0:T(256)S(1)} %get-tuple-element.13), channel_id=1, replica_groups=mesh['dp'=32,'tensor'=8] {'dp','tensor'}, use_global_device_ids=true, to_apply=%region_4.5 | all-reduce | flops 256 | bytes 2048 | tf_op jit(solution)/shard_map/pmax | solution.py:32
  217.0 0.2 fusion.3
  217.2 73.7 %all-reduce.2 = (f32[256]{0:T(256)S(1)}, f32[256]{0:T(256)S(1)}) all-reduce(f32[256]{0:T(256)S(1)} %get-tuple-element.3, f32[256]{0:T(256)S(1)} %get-tuple-element.2), channel_id=1, replica_groups=mesh['dp'=32,'tensor'=8] {'dp','tensor'}, use_global_device_ids=true, to_apply=%region_6.7 | all-reduce | flops 512 | bytes 4096 | tf_op jit(solution)/shard_map/psum | solution.py:34
  290.9 9.1 %fusion.4 = f32[256,8192]{1,0:T(8,128)} fusion(bf16[501,8192]{1,0:T(8,128)(2,1)} %param.6, f32[256,501]{0,1:T(8,128)S(1)} %get-tuple-element.14, s32[256]{0:T(256)S(1)} %all-reduce, f32[256]{0:T(256)S(1)} %get-tuple-element.10, s32[501]{0:T(512)S(1)} %iota_add_fusion, pred[256]{0:T(512)(128)(4,1)S(1)} %get-tuple-element.9), kind=kOutput, calls=%fused_computation.8 | convolution fusion | flops 2102115840 | bytes 17114324 | tf_op jit(solution)/shard_map/dot_general | solution.py:42
  300.1 0.6 dynamic_slice.5
  300.6 1.2 broadcast_select_fusion
  301.8 276.6 %all-reduce.5.cloned.1.call-done = f32[256,8192]{1,0:T(8,128)} async-done(((f32[256,8192]{1,0:T(8,128)}), f32[256,8192]{1,0:T(8,128)}) %all-reduce.5.cloned.1.call-update) | async-done | bytes 8388624
  578.4 1.0 dynamic-slice_multiply_fusion
  579.4 1.7 select_convert_fusion
  (6 shorter events, 0.0 us)
Async XLA Ops:
  7.2 3.2 copy-start
  7.2 121.7 %all-gather.3.cloned.1.call-start = ((), (), s32[]{:S(2)}) async-start(), calls=%async_computation | async-start | bytes 4210688 | tf_op jit(solution)/shard_map/all_gather | solution.py:21
  11.4 567.0 %all-reduce.5.cloned.1.call-start = ((), (), s32[]{:S(2)}) async-start(), calls=%async_computation.1 | async-start | bytes 16777216
Sparse Core Ops, SparseCore 0:
  12.3 116.5 all-gather.2
  300.2 278.2 all-reduce.4
where the time goes:
time: 589 us; the launch traced here: 588 us
  waiting for transfers between devices  314 us (53%)
  blocking collectives  227 us (39%)
  between operations  16.1 us (3%)
  matrix products  15.7 us (3%)
  local copies, waits for them, and re-layouts  8.79 us (1%)
  other arithmetic  6.82 us (1%)
    unnamed x3, waiting for transfers between devices  277 us
    unnamed x1, blocking collectives  78.3 us
    pmax x1, blocking collectives, shards(): row_top = lax.pmax(local_top, ('dp', 'tensor'))  74.6 us
    psum x1, blocking collectives, shards(): row_total, picked = lax.psum((shifted_total, local_pick), ('dp', 'tensor'))  73.7 us
    all_gather x1, waiting for transfers between devices, shards(): lax.all_gather(packed, ('dp', 'tensor'), axis=0, tiled=True)  37 us
  transfers between devices with their start and end apart: 2, of which 2 were waited for; matrix products, arithmetic and copies ran while one was open for 0% of the time, Pallas kernels for 0%

commit v1 on v0

--- a/solution.py
+++ b/solution.py
@@ -1,3 +1,4 @@
+import functools
 import jax
 import jax.numpy as jnp
 from jax import lax
@@ -5,6 +6,13 @@
 
 CAP = 1
 loss_scale = 128.0
+
+
+def expand_state(arr, ax_name, axis_name):
+    return jax.lax.psum(jax.lax.psum(arr, ax_name), axis_name)
+
+
+_find_views = functools.partial(expand_state, ax_name="dp", axis_name="tensor")
 
 
 def shards(hidden, out_weight, loss_mask, targets, kept_count):
@@ -31,7 +39,7 @@
     local_pick = jnp.sum(jnp.where(target_hit, logits, 0.0), axis=1)
     row_top = lax.pmax(local_top, ("dp", "tensor"))
     shifted_total = jnp.sum(jnp.exp(logits - row_top[:, None]), axis=1)
-    row_total, picked = lax.psum((shifted_total, local_pick), ("dp", "tensor"))
+    row_total, picked = _find_views((shifted_total, local_pick))
     log_total = row_top + jnp.log(row_total)
     slot_loss = jnp.where(filled, log_total - picked, 0.0)
     probabilities = jnp.exp(logits - log_total[:, None])

time: 589 us -> 592 us (level)
    psum x1 -> x2, blocking collectives: 73.7 us -> 74.7 us  [expand_state(): return jax.lax.psum(jax.lax.psum(arr, ax_name), axis_name)]
where the time goes in v1:
time: 592 us
  waiting for transfers between devices  316 us (53%)
  blocking collectives  228 us (39%)
  between operations  16.1 us (3%)
  matrix products  15.7 us (3%)
  local copies, waits for them, and re-layouts  8.79 us (1%)
  other arithmetic  6.83 us (1%)
    unnamed x3, waiting for transfers between devices  279 us
    unnamed x1, blocking collectives  78.3 us
    psum x2, blocking collectives, expand_state(): return jax.lax.psum(jax.lax.psum(arr, ax_name), axis_name)  74.7 us
    pmax x1, blocking collectives, shards(): row_top = lax.pmax(local_top, ('dp', 'tensor'))  74.6 us
    all_gather x1, waiting for transfers between devices, shards(): lax.all_gather(packed, ('dp', 'tensor'), axis=0, tiled=True)  37 us
  transfers between devices with their start and end apart: 2, of which 2 were waited for; matrix products, arithmetic and copies ran while one was open for 0% of the time, Pallas kernels for 0%

profile of v1, /device:TPU:97, one launch (start us, length us, event | category | flops | bytes accessed | tf_op | source)
XLA Modules:
  0.0 591.7 jit_solution(13067195894622638861)
XLA Ops:
  7.2 0.0 all-gather.3.cloned.1.call-start
  8.0 0.8 copy.9
  8.8 0.2 reduce-window.4
  8.9 0.1 compare_reduce_fusion
  9.1 1.3 select_reduce_fusion
  10.4 0.4 fusion.11
  10.8 0.6 convert_element_type.16
  11.4 0.0 all-reduce.6.cloned.1.call-start
  11.5 0.6 and_reduce_fusion
  13.4 0.1 dynamic-update-slice
  13.5 78.3 %all-reduce = s32[256]{0:T(256)S(1)} all-reduce(s32[256]{0:T(256)S(1)} %dynamic-update-slice), channel_id=1, replica_groups=mesh['dp'=32,'tensor'=8] {'dp','tensor'}, use_global_device_ids=true, to_apply=%add | all-reduce | flops 256 | bytes 2048
  91.8 37.0 %all-gather.3.cloned.1.call-done = bf16[2097152]{0:T(1024)(128)(2,1)} async-done(((bf16[8192]{0:T(1024)(128)(2,1)}), bf16[2097152]{0:T(1024)(128)(2,1)}) %all-gather.3.cloned.1.call-update) | async-done | bytes 4194320 | tf_op jit(solution)/shard_map/all_gather | solution.py:29
  128.9 7.3 %reshape.49 = bf16[256,8192]{1,0:T(8,128)(2,1)} reshape(bf16[2097152]{0:T(1024)(128)(2,1)} %all-gather.3.cloned.1.call-done) | data formatting | bytes 8388608 | tf_op jit(solution)/shard_map/all_gather | solution.py:29
  136.2 6.3 %fusion.15 = (f32[256]{0:T(256)S(1)}, f32[256,501]{0,1:T(8,128)S(1)}) fusion(bf16[256,8192]{1,0:T(8,128)(2,1)} %reshape.49, bf16[501,8192]{1,0:T(8,128)(2,1)} %param.6), kind=kOutput, calls=%fused_computation.29 | convolution fusion | flops 2101474304 | bytes 12916736 | tf_op jit(solution)/shard_map/rd,vd->rv/dot_general | solution.py:36
  142.4 74.6 %pmax.7 = f32[256]{0:T(256)S(1)} all-reduce(f32[256]{0:T(256)S(1)} %get-tuple-element.15), channel_id=1, replica_groups=mesh['dp'=32,'tensor'=8] {'dp','tensor'}, use_global_device_ids=true, to_apply=%region_4.5 | all-reduce | flops 256 | bytes 2048 | tf_op jit(solution)/shard_map/pmax | solution.py:40
  217.0 0.2 fusion.3
  217.2 62.7 %all-reduce.2 = (f32[256]{0:T(256)S(1)}, f32[256]{0:T(256)S(1)}) all-reduce(f32[256]{0:T(256)S(1)} %get-tuple-element.3, f32[256]{0:T(256)S(1)} %get-tuple-element.2), channel_id=1, replica_groups=mesh['dp'=32,'tensor'=8] {'dp'}, use_global_device_ids=true, to_apply=%region_6.7 | all-reduce | flops 512 | bytes 4096 | tf_op jit(solution)/shard_map/psum | solution.py:12
  279.9 12.0 %all-reduce.3 = (f32[256]{0:T(256)S(1)}, f32[256]{0:T(256)S(1)}) all-reduce(f32[256]{0:T(256)S(1)} %get-tuple-element.6, f32[256]{0:T(256)S(1)} %get-tuple-element.7), channel_id=1, replica_groups=mesh['dp'=32,'tensor'=8] {'tensor'}, use_global_device_ids=true, to_apply=%region_7.8 | all-reduce | flops 512 | bytes 4096 | tf_op jit(solution)/shard_map/psum | solution.py:12
  291.9 9.1 %fusion.4 = f32[256,8192]{1,0:T(8,128)} fusion(bf16[501,8192]{1,0:T(8,128)(2,1)} %param.6, f32[256,501]{0,1:T(8,128)S(1)} %get-tuple-element.16, s32[256]{0:T(256)S(1)} %all-reduce, f32[256]{0:T(256)S(1)} %get-tuple-element.12, s32[501]{0:T(512)S(1)} %iota_add_fusion, pred[256]{0:T(512)(128)(4,1)S(1)} %get-tuple-element.11), kind=kOutput, calls=%fused_computation.8 | convolution fusion | flops 2102115840 | bytes 17114324 | tf_op jit(solution)/shard_map/dot_general | solution.py:50
  301.0 0.6 dynamic_slice.5
  301.6 1.2 broadcast_select_fusion
  302.8 279.4 %all-reduce.6.cloned.1.call-done = f32[256,8192]{1,0:T(8,128)} async-done(((f32[256,8192]{1,0:T(8,128)}), f32[256,8192]{1,0:T(8,128)}) %all-reduce.6.cloned.1.call-update) | async-done | bytes 8388624
  582.2 1.0 dynamic-slice_multiply_fusion
  583.2 1.7 select_convert_fusion
  (7 shorter events, 0.1 us)
Async XLA Ops:
  7.2 3.2 copy-start
  7.2 121.7 %all-gather.3.cloned.1.call-start = ((), (), s32[]{:S(2)}) async-start(), calls=%async_computation | async-start | bytes 4210688 | tf_op jit(solution)/shard_map/all_gather | solution.py:29
  11.4 570.8 %all-reduce.6.cloned.1.call-start = ((), (), s32[]{:S(2)}) async-start(), calls=%async_computation.1 | async-start | bytes 16777216
Sparse Core Ops, SparseCore 0:
  12.3 116.5 all-gather.2
  301.2 281.0 all-reduce.5

commit v2 on v0

--- a/solution.py
+++ b/solution.py
@@ -5,6 +5,13 @@
 
 CAP = 1
 loss_scale = 128.0
+
+
+def all_by_exchange(value, axis, dim):
+    size = lax.axis_size(axis)
+    tiles = jnp.stack([value for _ in range(size)])
+    tiles = lax.all_to_all(tiles, axis, split_axis=0, concat_axis=0)
+    return jnp.concatenate(tiles, axis=dim)
 
 
 def shards(hidden, out_weight, loss_mask, targets, kept_count):
@@ -18,7 +25,7 @@
     slot_target = jnp.sum(jnp.where(slot_hits, targets[None, :], 0), axis=1)
     packed_target = jnp.where(jnp.any(slot_hits, axis=1), slot_target, -1)
     gathered, gathered_target = (
-        lax.all_gather(packed, ("dp", "tensor"), axis=0, tiled=True),
+        all_by_exchange(packed, ("dp", "tensor"), 0),
         lax.all_gather(packed_target, ("dp", "tensor"), axis=0, tiled=True),
     )
     filled = gathered_target >= 0

time: 589 us -> 686 us (1.16)
  blocking collectives: 227 us -> 281 us
  waiting for transfers between devices: 314 us -> 277 us
  local copies, waits for them, and re-layouts: 8.79 us -> 42 us
  other arithmetic: 6.82 us -> 33.1 us
  starting transfers between devices: 0.08 us -> 15.3 us
    unnamed x1, blocking collectives: 78.3 us -> 133 us
    all_gather x1 -> x0, waiting for transfers between devices: 37 us -> none  [shards(): lax.all_gather(packed, ('dp', 'tensor'), axis=0, tiled=True)]
    unnamed x4 -> x6, local copies, waits for them, and re-layouts: 0.13 us -> 34.5 us
    another operation x1 -> x2, other arithmetic: 0.17 us -> 27 us  [the longest x1 26.9 us: all_by_exchange(): tiles = jnp.stack([value for _ in range(size)])]
    all_to_all x0 -> x1, starting transfers between devices: none -> 15.3 us  [all_by_exchange(): tiles = lax.all_to_all(tiles, axis, split_axis=0, concat_axis=0)]
    all_gather x1 -> x0, local copies, waits for them, and re-layouts: 7.31 us -> none  [shards(): lax.all_gather(packed, ('dp', 'tensor'), axis=0, tiled=True)]
    unnamed x3 -> x2, waiting for transfers between devices: 277 us -> 277 us
  transfers between devices with their start and end apart: 2 -> 2, of which waited for: 2 -> 1; matrix products, arithmetic and copies ran while one was open for 0% -> 0% of each run, Pallas kernels for 0% -> 0%
where the time goes in v2:
time: 686 us; the launch traced here: 685 us
  blocking collectives  281 us (41%)
  waiting for transfers between devices  277 us (40%)
  local copies, waits for them, and re-layouts  42 us (6%)
  other arithmetic  33.1 us (5%)
  matrix products  20.9 us (3%)
  between operations  16.2 us (2%)
  starting transfers between devices  15.3 us (2%)
    unnamed x2, waiting for transfers between devices  277 us
    unnamed x1, blocking collectives  133 us
    psum x1, blocking collectives, shards(): row_total, picked = lax.psum((shifted_total, local_pick), ('dp', 'tensor'))  74.1 us
    pmax x1, blocking collectives, shards(): row_top = lax.pmax(local_top, ('dp', 'tensor'))  73.5 us
    unnamed x6, local copies, waits for them, and re-layouts  34.5 us
    another operation x1, other arithmetic, all_by_exchange(): tiles = jnp.stack([value for _ in range(size)])  26.9 us
    all_to_all x1, starting transfers between devices, all_by_exchange(): tiles = lax.all_to_all(tiles, axis, split_axis=0, concat_axis=0)  15.3 us
  transfers between devices with their start and end apart: 2, of which 1 were waited for; matrix products, arithmetic and copies ran while one was open for 0% of the time, Pallas kernels for 0%

profile of v2, /device:TPU:97, one launch (start us, length us, event | category | flops | bytes accessed | tf_op | source)
XLA Modules:
  0.0 684.7 jit_solution(1338794455101952133)
XLA Ops:
  8.0 0.8 copy.9
  8.7 0.2 reduce-window.4
  8.9 0.1 compare_reduce_fusion
  9.0 1.3 select_reduce_fusion
  10.3 0.4 fusion.14
  10.7 5.6 stack.2
  16.4 0.5 broadcast.62
  16.9 26.9 %reduce.8 = bf16[256,8192]{1,0:T(8,128)(2,1)} reduce(bf16[256,1,8192]{2,1,0:T(2,128)(2,1)} %stack.2, bf16[]{:T(256)} %broadcast.62), dimensions={1}, to_apply=%stack.2.reduce_sub_computation | reduce | bytes 8388610 | tf_op jit(solution)/shard_map/stack | solution.py:12
  43.7 7.8 %reshape.62 = bf16[256,2,4096]{2,1,0:T(2,128)(2,1)} reshape(bf16[256,8192]{1,0:T(8,128)(2,1)} %reduce.8) | data formatting | bytes 8388608
  51.5 15.3 %all-to-all-start = ((bf16[256,2,4096]{2,1,0:T(2,128)(2,1)}), bf16[256,2,4096]{2,1,0:T(2,128)(2,1)}, u32[]{:S(2)}, u32[]{:S(2)}) async-start(bf16[256,2,4096]{2,1,0:T(2,128)(2,1)} %reshape.62), calls=%async_computation | async-start | bytes 8388608 | tf_op jit(solution)/shard_map/all_to_all | solution.py:13
  66.9 0.6 and_reduce_fusion
  68.9 0.1 dynamic-update-slice
  69.0 132.9 %all-reduce = s32[256]{0:T(256)S(1)} all-reduce(s32[256]{0:T(256)S(1)} %dynamic-update-slice), channel_id=1, replica_groups=mesh['dp'=32,'tensor'=8] {'dp','tensor'}, use_global_device_ids=true, to_apply=%add | all-reduce | flops 256 | bytes 2048
  201.9 26.6 %reshape.63 = bf16[256,1,8192]{2,1,0:T(2,128)(2,1)} reshape(bf16[256,2,4096]{2,1,0:T(2,128)(2,1)} %all-to-all-done) | data formatting | bytes 8388608
  228.5 11.4 %fusion.18 = (f32[256]{0:T(256)S(1)}, f32[256,501]{0,1:T(8,128)S(1)}) fusion(bf16[501,8192]{1,0:T(8,128)(2,1)} %param.6, bf16[256,1,8192]{2,1,0:T(2,128)(2,1)} %reshape.63), kind=kOutput, calls=%fused_computation.32 | convolution fusion | flops 2101474304 | bytes 12916736 | tf_op jit(solution)/shard_map/rd,vd->rv/dot_general | solution.py:35
  239.9 73.5 %pmax.7 = f32[256]{0:T(256)S(1)} all-reduce(f32[256]{0:T(256)S(1)} %get-tuple-element.13), channel_id=1, replica_groups=mesh['dp'=32,'tensor'=8] {'dp','tensor'}, use_global_device_ids=true, to_apply=%region_4.5 | all-reduce | flops 256 | bytes 2048 | tf_op jit(solution)/shard_map/pmax | solution.py:39
  313.4 0.2 fusion.6
  313.5 74.1 %all-reduce.2 = (f32[256]{0:T(256)S(1)}, f32[256]{0:T(256)S(1)}) all-reduce(f32[256]{0:T(256)S(1)} %get-tuple-element.3, f32[256]{0:T(256)S(1)} %get-tuple-element.2), channel_id=1, replica_groups=mesh['dp'=32,'tensor'=8] {'dp','tensor'}, use_global_device_ids=true, to_apply=%region_6.7 | all-reduce | flops 512 | bytes 4096 | tf_op jit(solution)/shard_map/psum | solution.py:41
  387.6 9.1 %fusion.7 = f32[256,8192]{1,0:T(8,128)} fusion(bf16[501,8192]{1,0:T(8,128)(2,1)} %param.6, f32[256,501]{0,1:T(8,128)S(1)} %get-tuple-element.14, s32[256]{0:T(256)S(1)} %all-reduce, f32[256]{0:T(256)S(1)} %get-tuple-element.10, s32[501]{0:T(512)S(1)} %iota_add_fusion, pred[256]{0:T(512)(128)(4,1)S(1)} %get-tuple-element.9), kind=kOutput, calls=%fused_computation.11 | convolution fusion | flops 2102115840 | bytes 17114324 | tf_op jit(solution)/shard_map/dot_general | solution.py:49
  396.8 0.6 dynamic_slice.5
  397.3 1.2 broadcast_select_fusion
  398.5 276.7 %all-reduce.5.cloned.1.call-done = f32[256,8192]{1,0:T(8,128)} async-done(((f32[256,8192]{1,0:T(8,128)}), f32[256,8192]{1,0:T(8,128)}) %all-reduce.5.cloned.1.call-update) | async-done | bytes 8388624
  675.2 1.0 dynamic-slice_multiply_fusion
  676.1 1.7 select_convert_fusion
  (9 shorter events, 0.1 us)
Async XLA Ops:
  7.2 3.2 copy-start
  51.5 150.4 %all-to-all-start = ((bf16[256,2,4096]{2,1,0:T(2,128)(2,1)}), bf16[256,2,4096]{2,1,0:T(2,128)(2,1)}, u32[]{:S(2)}, u32[]{:S(2)}) async-start(bf16[256,2,4096]{2,1,0:T(2,128)(2,1)} %reshape.62), calls=%async_computation | async-start | bytes 8388608 | tf_op jit(solution)/shard_map/all_to_all | solution.py:13
  66.8 608.3 %all-reduce.5.cloned.1.call-start = ((), (), s32[]{:S(2)}) async-start(), calls=%async_computation.1 | async-start | bytes 16777216
Sparse Core Ops, SparseCore 0:
  396.9 278.2 all-reduce.4
